TPU v7x, 32 devices: a whole 2x2x4 slice. The times are simulated.
32 devices in a mesh: gx: 8 (over z, y), gy: 4 (over x, core).
Axes of the slice: x: 2, y: 2, z: 4, core: 2. Of those that a mesh axis runs over, the one named last changes fastest.
Arguments:
- positions: float32 [3, 8192, 128], P(None, ('gx', 'gy')), may hold values from 0 to 1
- masses: float32 [8192, 128], P(('gx', 'gy')), may hold values from 0.004 to 0.012
- smoothing: float32 [8192, 128], P(('gx', 'gy')), may hold values from 0.55 to 1
- entropy: float32 [8192, 128], P(('gx', 'gy')), may hold values from 0.5 to 2
- density: float32 [8192, 128], P(('gx', 'gy')), may hold values from 0.5 to 2
- active_cells: int32 [128], P(('gx', 'gy')), may hold values from 0 to 8191, as said below
- active_count: int32 [32], P(('gx', 'gy')), may hold values from 1 to 4, 84 in all
- neighbours: int32 [128, 27], P(('gx', 'gy')), may hold values from 0 to 8191, as said below
- mig_source: int32 [4096], P(('gx', 'gy')), may hold values from 0 to 32767
- mig_dest: int32 [4096, 1], P(('gx', 'gy')), may hold values from 0 to 31; in each aligned block of 128 rows (0 to 127, 128 to 255, ...) at most 8 rows name the same one
Outputs:
- new_density: float32 [8192, 128], P(('gx', 'gy'))
- acceleration: float32 [3, 128, 128], P(None, ('gx', 'gy'))
- arrivals: float32 [7, 8192], P(None, ('gx', 'gy'))
Inputs may be any that keep to these rules, and one draw needn't show every extreme that they name: `active_cells`: the 4 entries of device d are distinct cells of device d. The middle entry (index 13) of a slot is its active cell. Every other entry is a cell of the slot's own device, or a cell of the device just before or just after it in the cell order lying within 64 cells of the end they share. Over all slots of one device, at most 8 distinct cells of each of these two devices are named, and every device with neighbours on both sides names exactly 8 on each side. `mig_dest`: within the 128 rows of one device no destination appears more than 8 times; some destination appears exactly 8 times.
All inputs are finite; a program needn't handle non-finite values. No bound on the sum of `active_count` on one device may be relied on, other than what follows from the above.
Results may differ from a plain program's by a relative error of at most 0.0003.
Values sent between devices are 32-bit elements; how exact they have to be, the bound alone decides.
No kernel may reach another device: no remote copies, remote signals or barrier semaphores. Data moves between devices by JAX's collectives and lax.ppermute only.
A program may use at most 64 MiB of HBM per device.

v0:
```python
import math
import jax
import jax.numpy as jnp
from jax import lax
from jax.sharding import PartitionSpec as P

P_SIZE = 128
NBR = 27
RIM = 64
kernel_norm = 8.0 / math.pi


def padded(block, sides, width):
    for axis, dim in sides:
        count = lax.axis_size(axis)
        forward = [(i, i + 1) for i in range(count - 1)]
        backward = [(target, source) for source, target in forward]
        low = lax.ppermute(
            lax.slice_in_dim(block, block.shape[dim] - width, None, axis=dim), axis, forward
        )
        high = lax.ppermute(lax.slice_in_dim(block, 0, width, axis=dim), axis, backward)
        block = jnp.concatenate([low, block, high], axis=dim)
    return block


def stencil_offsets():
    index = jnp.arange(NBR)
    return jnp.stack([index // 9 - 1, index // 3 % 3 - 1, index % 3 - 1]).astype(jnp.float32)


def kernel_value(ratio):
    inner = 1.0 - 6.0 * ratio * ratio + 6.0 * ratio * ratio * ratio
    outer = 2.0 * (1.0 - ratio) ** 3
    return jnp.where(ratio < 0.5, inner, jnp.where(ratio < 1.0, outer, 0.0))


def kernel_slope(ratio):
    safe_ratio = jnp.maximum(ratio, 0.5)
    inner = -12.0 + 18.0 * ratio
    outer = -6.0 * (1.0 - ratio) ** 2 / safe_ratio
    return jnp.where(ratio < 0.5, inner, jnp.where(ratio < 1.0, outer, 0.0))


def pair_geometry(own_pos, other_pos):
    separation = own_pos[:, :, None, None] - other_pos[:, None, :, :]
    distance = jnp.sqrt(jnp.sum(separation * separation, axis=0))
    return (separation, distance)


def density_cell(own_pos, own_len, other_pos, other_mass):
    separation, distance = pair_geometry(own_pos, other_pos)
    weights = kernel_value(distance / own_len[:, None, None])
    return kernel_norm * jnp.sum(other_mass[None] * weights, axis=(1, 2)) / own_len**3


def force_cell(
    own_pos, own_len, own_rho, own_press, other_pos, other_mass, other_len, other_rho, other_press
):
    separation, distance = pair_geometry(own_pos, other_pos)
    own_term = (own_press / own_rho**2 * kernel_norm / own_len**5)[
        :, None, None
    ] * kernel_slope(distance / own_len[:, None, None])
    other_term = (other_press / other_rho**2 * kernel_norm / other_len**5)[None] * kernel_slope(
        distance / other_len[None]
    )
    factor = other_mass[None] * (own_term + other_term)
    return -jnp.sum(factor[None] * separation, axis=(2, 3))


def gather_slots(table_pos, lookup_ids, stencil):
    near_pos = jnp.take(table_pos, lookup_ids, axis=1) + stencil[:, None, :, None]
    return jnp.moveaxis(near_pos, 1, 0)


def local(
    positions,
    masses,
    smoothing,
    entropy,
    density,
    active_cells,
    active_count,
    neighbours,
    mig_source,
    mig_dest,
):
    cell_count = masses.shape[0]
    slot_count = active_cells.shape[0]
    my_index = lax.axis_index(("gx", "gy"))
    devices = lax.axis_size(("gx", "gy"))
    stencil = stencil_offsets()
    local_active = active_cells - my_index * cell_count
    near_index = neighbours - (my_index * cell_count - RIM)
    live_slot = jnp.arange(slot_count) < active_count[0]
    first_rows = jnp.concatenate([positions, masses[None]], axis=0)
    extended = padded(first_rows, ((("gx", "gy"), 1),), RIM)
    own_pos = jnp.moveaxis(jnp.take(positions, local_active, axis=1), 1, 0)
    own_len = smoothing[local_active]
    near_pos = gather_slots(extended[0:3], near_index, stencil)
    near_mass = extended[3][near_index]

    def density_one(inputs):
        cell_pos, cell_len, other_pos, other_mass = inputs
        return density_cell(cell_pos, cell_len, other_pos, other_mass)

    rho = lax.map(density_one, (own_pos, own_len, near_pos, near_mass))
    kept = jnp.where(live_slot[:, None], rho, density[local_active])
    new_density = density.at[local_active].set(kept)
    pressure = entropy * jnp.exp(5.0 / 3.0 * jnp.log(new_density))
    state_rows = jnp.concatenate(
        [positions, masses[None], smoothing[None], new_density[None], pressure[None]], axis=0
    )
    ghost_all = padded(state_rows, ((("gx", "gy"), 1),), RIM)
    force_pos = gather_slots(ghost_all[0:3], near_index, stencil)
    force_mass = ghost_all[3][near_index]
    force_len = ghost_all[4][near_index]
    force_rho = ghost_all[5][near_index]
    force_press = ghost_all[6][near_index]
    own_rho = new_density[local_active]
    own_press = pressure[local_active]

    def force_one(inputs):
        (
            cell_pos,
            cell_len,
            cell_rho,
            cell_press,
            other_pos,
            other_mass,
            other_len,
            other_rho,
            other_press,
        ) = inputs
        return force_cell(
            cell_pos,
            cell_len,
            cell_rho,
            cell_press,
            other_pos,
            other_mass,
            other_len,
            other_rho,
            other_press,
        )

    accel_rows = lax.map(
        force_one,
        (
            own_pos,
            own_len,
            own_rho,
            own_press,
            force_pos,
            force_mass,
            force_len,
            force_rho,
            force_press,
        ),
    )
    acceleration = jnp.transpose(accel_rows, (1, 0, 2)) * live_slot[None, :, None].astype(
        jnp.float32
    )
    mig_rows = mig_source.shape[0]
    capacity = max(2, 2 * mig_rows // devices)
    flat_count = cell_count * P_SIZE
    payload = jnp.concatenate(
        [
            positions.reshape(3, flat_count)[:, mig_source],
            masses.reshape(flat_count)[mig_source][None],
            smoothing.reshape(flat_count)[mig_source][None],
            entropy.reshape(flat_count)[mig_source][None],
            new_density.reshape(flat_count)[mig_source][None],
        ],
        axis=0,
    )
    destination = mig_dest[:, 0]
    same = destination[:, None] == destination[None, :]
    earlier = jnp.arange(mig_rows)[None, :] < jnp.arange(mig_rows)[:, None]
    slot_rank = jnp.sum(jnp.logical_and(same, earlier), axis=1)
    column = destination * capacity + slot_rank
    outgoing = jnp.zeros((7, devices * capacity), jnp.float32).at[:, column].set(payload)
    arrivals = lax.all_to_all(outgoing, ("gx", "gy"), split_axis=1, concat_axis=1, tiled=True)
    return (new_density, acceleration, arrivals)


def solution(mesh):
    placed = (
        P(None, ("gx", "gy"), None),
        P(("gx", "gy"), None),
        P(("gx", "gy"), None),
        P(("gx", "gy"), None),
        P(("gx", "gy"), None),
        P(("gx", "gy")),
        P(("gx", "gy")),
        P(("gx", "gy"), None),
        P(("gx", "gy")),
        P(("gx", "gy"), None),
    )
    return jax.shard_map(
        local,
        mesh=mesh,
        in_specs=placed,
        out_specs=(P(("gx", "gy"), None), P(None, ("gx", "gy"), None), P(None, ("gx", "gy"))),
        check_vma=False,
    )
```

profile of v0, /device:TPU:0, one launch (start us, length us, event | category | flops | bytes accessed | tf_op | source)
XLA Modules:
  0.0 87.4 jit_solution(12953888744872572733)
XLA Ops:
  0.7 1.1 %pad_maximum_fusion.5 = (f32[4,64,128]{2,1,0:T(8,128)S(1)}, f32[4,64,128]{2,1,0:T(8,128)S(1)}) fusion(f32[1,256,128]{2,1,0:T(8,128)} %bitcast.109, f32[3,256,128]{2,1,0:T(8,128)} %param.16), kind=kLoop, calls=%fused_computation.73 | loop fusion | flops 65536 | bytes 786432 | tf_op jit(solution)/shard_map/slice | solution.py:19
  1.8 2.4 %collective-permute-start = (f32[4,64,128]{2,1,0:T(8,128)S(1)}, f32[4,64,128]{2,1,0:T(8,128)S(1)}, u32[]{:S(2)}, u32[]{:S(2)}) collective-permute-start(f32[4,64,128]{2,1,0:T(8,128)S(1)} %get-tuple-element.197), channel_id=1, source_target_pairs={{0,1},{1,2},{2,3},{3,4},{4,5},{5,6},{6,7},{7,8},{8,9},{9,10},{10,1... | collective-permute-start | bytes 393224 | tf_op jit(solution)/shard_map/ppermute | solution.py:18
  4.2 1.3 %collective-permute-start.1 = (f32[4,64,128]{2,1,0:T(8,128)S(1)}, f32[4,64,128]{2,1,0:T(8,128)S(1)}, u32[]{:S(2)}, u32[]{:S(2)}) collective-permute-start(f32[4,64,128]{2,1,0:T(8,128)S(1)} %get-tuple-element.198), channel_id=1, source_target_pairs={{1,0},{2,1},{3,2},{4,3},{5,4},{6,5},{7,6},{8,7},{9,8},{10,9},{11,1... | collective-permute-start | bytes 393224 | tf_op jit(solution)/shard_map/ppermute | solution.py:21
  5.5 1.0 %constant_dynamic-update-slice_fusion.1 = f32[7,256,128]{2,1,0:T(8,128)S(1)} fusion(f32[3,256,128]{2,1,0:T(8,128)} %param.16), kind=kLoop, calls=%fused_computation.84 | loop fusion | bytes 786432
  8.7 8.7 %copy.60 = f32[3,256,128]{0,2,1:T(8,128)} copy(f32[3,256,128]{2,1,0:T(8,128)S(1)} %copy-done) | data formatting | bytes 786432 | tf_op args[0]
  17.4 6.4 %gather_fusion.9 = f32[128,3]{1,0:T(8,128)S(1)} fusion(f32[3,32768]{0,1:T(8,128)} %bitcast.107, s32[1024]{0:T(1024)S(1)} %pad_clamp_fusion), kind=kCustom, calls=%fused_computation.12 | custom fusion | bytes 3584 | tf_op jit(solution)/shard_map/gather | solution.py:168
  23.9 1.2 %gather_fusion.10 = f32[128]{0:T(128)S(1)} fusion(f32[32768]{0:T(1024)S(1)} %bitcast.110, s32[1024]{0:T(1024)S(1)} %pad_clamp_fusion), kind=kCustom, calls=%fused_computation.13 | custom fusion | bytes 1536 | tf_op jit(solution)/shard_map/gather | solution.py:169
  25.0 1.1 %gather_fusion.11 = f32[128]{0:T(128)S(1)} fusion(f32[32768]{0:T(1024)S(1)} %bitcast.113, s32[1024]{0:T(1024)S(1)} %pad_clamp_fusion), kind=kCustom, calls=%fused_computation.14 | custom fusion | bytes 1536 | tf_op jit(solution)/shard_map/gather | solution.py:170
  26.2 1.1 %gather_fusion.12 = f32[128]{0:T(128)S(1)} fusion(f32[32768]{0:T(1024)S(1)} %bitcast.114, s32[1024]{0:T(1024)S(1)} %pad_clamp_fusion), kind=kCustom, calls=%fused_computation.15 | custom fusion | bytes 1536 | tf_op jit(solution)/shard_map/gather | solution.py:171
  28.0 0.7 gather_fusion.14
  29.5 9.0 %while.20 = (s32[]{:T(128)}, f32[4,128]{1,0:T(4,128)S(1)}, f32[4,27,128]{2,1,0:T(8,128)S(1)}, f32[4,3,128]{2,1,0:T(4,128)S(1)}, f32[4,3,27,128]{3,2,0,1:T(8,128)...) while((s32[]{:T(128)}, f32[4,128]{1,0:T(4,128)S(1)}, f32[4,27,128]{2,1,0:T(8,128)S(1)}, ...), condition=%wide.region_3.5_spmd, body=%wide.region_0.4_spmd.sunk | while | flops 10617218 | bytes 3714157 | solution.py:106
  30.3 1.4 %fusion.40 = f32[128]{0:T(128)S(1)} fusion(f32[128,27,128]{2,0,1:T(8,128)S(1)} %multiply_reduce_fusion.2, f32[128]{0:T(128)S(1)} %fusion.39, f32[27,128]{1,0:T(8,128)S(1)} %dynamic-slice_bitcast_fusion.12), kind=kLoop, calls=%fused_computation.27.clone.1 | loop fusion | flops 7077760 | bytes 1784320 | tf_op jit(solution)/shard_map/while/body/eval_jaxpr/reduce_sum | solution.py:53
  32.6 1.4 %fusion.40 = f32[128]{0:T(128)S(1)} fusion(f32[128,27,128]{2,0,1:T(8,128)S(1)} %multiply_reduce_fusion.2, f32[128]{0:T(128)S(1)} %fusion.39, f32[27,128]{1,0:T(8,128)S(1)} %dynamic-slice_bitcast_fusion.12), kind=kLoop, calls=%fused_computation.27.clone.1 | loop fusion | flops 7077760 | bytes 1784320 | tf_op jit(solution)/shard_map/while/body/eval_jaxpr/reduce_sum | solution.py:53
  34.8 1.4 %fusion.40 = f32[128]{0:T(128)S(1)} fusion(f32[128,27,128]{2,0,1:T(8,128)S(1)} %multiply_reduce_fusion.2, f32[128]{0:T(128)S(1)} %fusion.39, f32[27,128]{1,0:T(8,128)S(1)} %dynamic-slice_bitcast_fusion.12), kind=kLoop, calls=%fused_computation.27.clone.1 | loop fusion | flops 7077760 | bytes 1784320 | tf_op jit(solution)/shard_map/while/body/eval_jaxpr/reduce_sum | solution.py:53
  37.1 1.4 %fusion.40 = f32[128]{0:T(128)S(1)} fusion(f32[128,27,128]{2,0,1:T(8,128)S(1)} %multiply_reduce_fusion.2, f32[128]{0:T(128)S(1)} %fusion.39, f32[27,128]{1,0:T(8,128)S(1)} %dynamic-slice_bitcast_fusion.12), kind=kLoop, calls=%fused_computation.27.clone.1 | loop fusion | flops 7077760 | bytes 1784320 | tf_op jit(solution)/shard_map/while/body/eval_jaxpr/reduce_sum | solution.py:53
  38.6 0.7 scatter_custom_fusion
  39.4 5.1 %collective-permute-start.2 = (f32[7,64,128]{2,1,0:T(8,128)S(1)}, f32[7,64,128]{2,1,0:T(8,128)S(1)}, u32[]{:S(2)}, u32[]{:S(2)}) collective-permute-start(f32[7,64,128]{2,1,0:T(8,128)S(1)} %get-tuple-element.195), channel_id=1, source_target_pairs={{0,1},{1,2},{2,3},{3,4},{4,5},{5,6},{6,7},{7,8},{8,9},{9,10},{10,1... | collective-permute-start | bytes 688136 | tf_op jit(solution)/shard_map/ppermute | solution.py:18
  44.6 1.3 %collective-permute-start.3 = (f32[7,64,128]{2,1,0:T(8,128)S(1)}, f32[7,64,128]{2,1,0:T(8,128)S(1)}, u32[]{:S(2)}, u32[]{:S(2)}) collective-permute-start(f32[7,64,128]{2,1,0:T(8,128)S(1)} %get-tuple-element.196), channel_id=1, source_target_pairs={{1,0},{2,1},{3,2},{4,3},{5,4},{6,5},{7,6},{8,7},{9,8},{10,9},{11,1... | collective-permute-start | bytes 688136 | tf_op jit(solution)/shard_map/ppermute | solution.py:21
  45.9 1.1 %gather_fusion.13 = f32[128]{0:T(128)S(1)} fusion(f32[32768]{0:T(1024)S(1)} %bitcast.108, s32[1024]{0:T(1024)S(1)} %pad_clamp_fusion), kind=kCustom, calls=%fused_computation.16 | custom fusion | bytes 1536 | tf_op jit(solution)/shard_map/gather | solution.py:172
  47.2 0.9 %scatter_custom_fusion.1 = f32[7,256]{0,1:T(8,128)S(1)} fusion(s32[128]{0:T(128)S(1)} %fusion.28, f32[128,7]{1,0:T(8,128)S(1)} %copy.62, f32[]{:T(128)} %constant.137.clone.1), kind=kCustom, calls=%fused_computation.80 | custom fusion | bytes 7172 | tf_op jit(solution)/shard_map/scatter | solution.py:181
  48.1 0.9 %copy.63 = f32[7,32,8]{2,0,1:T(8,128)} copy(f32[7,32,8]{0,2,1:T(8,128)S(1)} %bitcast.117) | data formatting | bytes 14336 | tf_op jit(solution)/shard_map/all_to_all | solution.py:182
  49.0 10.0 %all-to-all-start = ((f32[7,32,8]{2,0,1:T(8,128)}), f32[7,32,8]{2,0,1:T(8,128)S(1)}, u32[]{:S(2)}, u32[]{:S(2)}) async-start(f32[7,32,8]{2,0,1:T(8,128)} %copy.63), calls=%async_computation | async-start | bytes 262144 | tf_op jit(solution)/shard_map/all_to_all | solution.py:182
  60.2 7.1 %all-to-all-done = f32[7,32,8]{2,0,1:T(8,128)S(1)} async-done(((f32[7,32,8]{2,0,1:T(8,128)}), f32[7,32,8]{2,0,1:T(8,128)S(1)}, u32[]{:S(2)}, u32[]{:S(2)}) %all-to-all-start) | async-done | bytes 7200 | tf_op jit(solution)/shard_map/all_to_all | solution.py:182
  67.3 0.7 all_to_all.10
  68.6 0.7 gather_fusion.15
  72.0 14.6 %while.21 = (s32[]{:T(128)}, f32[4,3,128]{2,0,1:T(4,128)S(1)}, f32[4,27,128]{2,1,0:T(8,128)S(1)}, f32[4,128]{1,0:T(4,128)S(1)}, f32[4,128]{1,0:T(4,128)S(1)}, /*...) while((s32[]{:T(128)}, f32[4,3,128]{2,0,1:T(4,128)S(1)}, ...), condition=%wide.region_8.10_spmd, body=%wide.region_5.9_spmd.sunk | while | flops 19931648 | bytes 7402641 | solution.py:146
  72.8 2.1 %add_multiply_fusion.2 = f32[128,27,128]{2,0,1:T(8,128)S(1)} fusion(f32[128,27,128]{2,0,1:T(8,128)S(1)} %fusion.43, f32[27,128]{1,0:T(8,128)S(1)} %get-tuple-element.312, f32[27,128]{1,0:T(8,128)S(1)} %get-tuple-element.313, f32[128]{0:T(128)S(1)} %get-tuple-element.314, f32[128]{0:T(128)S(1)} %get-tuple-element.315, f32[27,128]{1,0:T(8,128)S(1)} %get-tuple-element.316), kind=kLoop, calls=%fused_computation.42.clone.1 | loop fusion | flops 12386304 | bytes 3581440 | tf_op jit(solution)/shard_map/while/body/eval_jaxpr/mul | solution.py:66
  75.0 0.7 fusion.44
  76.5 2.1 %add_multiply_fusion.2 = f32[128,27,128]{2,0,1:T(8,128)S(1)} fusion(f32[128,27,128]{2,0,1:T(8,128)S(1)} %fusion.43, f32[27,128]{1,0:T(8,128)S(1)} %get-tuple-element.312, f32[27,128]{1,0:T(8,128)S(1)} %get-tuple-element.313, f32[128]{0:T(128)S(1)} %get-tuple-element.314, f32[128]{0:T(128)S(1)} %get-tuple-element.315, f32[27,128]{1,0:T(8,128)S(1)} %get-tuple-element.316), kind=kLoop, calls=%fused_computation.42.clone.1 | loop fusion | flops 12386304 | bytes 3581440 | tf_op jit(solution)/shard_map/while/body/eval_jaxpr/mul | solution.py:66
  78.6 0.7 fusion.44
  80.1 2.1 %add_multiply_fusion.2 = f32[128,27,128]{2,0,1:T(8,128)S(1)} fusion(f32[128,27,128]{2,0,1:T(8,128)S(1)} %fusion.43, f32[27,128]{1,0:T(8,128)S(1)} %get-tuple-element.312, f32[27,128]{1,0:T(8,128)S(1)} %get-tuple-element.313, f32[128]{0:T(128)S(1)} %get-tuple-element.314, f32[128]{0:T(128)S(1)} %get-tuple-element.315, f32[27,128]{1,0:T(8,128)S(1)} %get-tuple-element.316), kind=kLoop, calls=%fused_computation.42.clone.1 | loop fusion | flops 12386304 | bytes 3581440 | tf_op jit(solution)/shard_map/while/body/eval_jaxpr/mul | solution.py:66
  83.8 2.1 %add_multiply_fusion.2 = f32[128,27,128]{2,0,1:T(8,128)S(1)} fusion(f32[128,27,128]{2,0,1:T(8,128)S(1)} %fusion.43, f32[27,128]{1,0:T(8,128)S(1)} %get-tuple-element.312, f32[27,128]{1,0:T(8,128)S(1)} %get-tuple-element.313, f32[128]{0:T(128)S(1)} %get-tuple-element.314, f32[128]{0:T(128)S(1)} %get-tuple-element.315, f32[27,128]{1,0:T(8,128)S(1)} %get-tuple-element.316), kind=kLoop, calls=%fused_computation.42.clone.1 | loop fusion | flops 12386304 | bytes 3581440 | tf_op jit(solution)/shard_map/while/body/eval_jaxpr/mul | solution.py:66
  (136 shorter events, 15.7 us)
Async XLA Ops:
  0.6 6.1 %copy-start = (f32[3,256,128]{2,1,0:T(8,128)S(1)}, f32[3,256,128]{2,1,0:T(8,128)}, u32[]{:S(2)}) copy-start(f32[3,256,128]{2,1,0:T(8,128)} %param.16) | copy-start | bytes 1179652
  0.6 7.3 %copy-start.3 = (f32[256,128]{1,0:T(8,128)S(1)}, f32[256,128]{1,0:T(8,128)}, u32[]{:S(2)}) copy-start(f32[256,128]{1,0:T(8,128)} %param.17) | copy-start | bytes 393220
  0.7 7.4 %copy-start.4 = (f32[256,128]{1,0:T(8,128)S(1)}, f32[256,128]{1,0:T(8,128)}, u32[]{:S(2)}) copy-start(f32[256,128]{1,0:T(8,128)} %param.18) | copy-start | bytes 393220
  0.7 5.9 %copy-start.7 = (s32[4]{0:T(128)S(1)}, s32[4]{0:T(128)}, u32[]{:S(2)}) copy-start(s32[4]{0:T(128)} %param.21) | copy-start | bytes 52
  0.7 5.9 %copy-start.6 = (s32[4,27]{1,0:T(4,128)S(1)}, s32[4,27]{1,0:T(4,128)}, u32[]{:S(2)}) copy-start(s32[4,27]{1,0:T(4,128)} %param.23) | copy-start | bytes 1300
  0.7 7.3 %copy-start.8 = (s32[128]{0:T(128)S(1)}, s32[128]{0:T(128)}, u32[]{:S(2)}) copy-start(s32[128]{0:T(128)} %param.24) | copy-start | bytes 1540
  1.8 25.8 %collective-permute-start = (f32[4,64,128]{2,1,0:T(8,128)S(1)}, f32[4,64,128]{2,1,0:T(8,128)S(1)}, u32[]{:S(2)}, u32[]{:S(2)}) collective-permute-start(f32[4,64,128]{2,1,0:T(8,128)S(1)} %get-tuple-element.197), channel_id=1, source_target_pairs={{0,1},{1,2},{2,3},{3,4},{4,5},{5,6},{6,7},{7,8},{8,9},{9,10},{10,1... | collective-permute-start | bytes 393224 | tf_op jit(solution)/shard_map/ppermute | solution.py:18
  4.2 23.4 %collective-permute-start.1 = (f32[4,64,128]{2,1,0:T(8,128)S(1)}, f32[4,64,128]{2,1,0:T(8,128)S(1)}, u32[]{:S(2)}, u32[]{:S(2)}) collective-permute-start(f32[4,64,128]{2,1,0:T(8,128)S(1)} %get-tuple-element.198), channel_id=1, source_target_pairs={{1,0},{2,1},{3,2},{4,3},{5,4},{6,5},{7,6},{8,7},{9,8},{10,9},{11,1... | collective-permute-start | bytes 393224 | tf_op jit(solution)/shard_map/ppermute | solution.py:21
  8.7 17.5 %copy-start.5 = (f32[256,128]{1,0:T(8,128)S(1)}, f32[256,128]{1,0:T(8,128)}, u32[]{:S(2)}) copy-start(f32[256,128]{1,0:T(8,128)} %param.19) | copy-start | bytes 393220
  8.7 18.7 %copy-start.9 = (s32[128,1]{0,1:T(1,128)S(1)}, s32[128,1]{0,1:T(1,128)}, u32[]{:S(2)}) copy-start(s32[128,1]{0,1:T(1,128)} %param.25) | copy-start | bytes 1540
  29.5 9.0 %copy-start.2 = (f32[256,128]{1,0:T(8,128)S(1)}, f32[256,128]{1,0:T(8,128)}, u32[]{:S(2)}) copy-start(f32[256,128]{1,0:T(8,128)} %param.20) | copy-start | bytes 393220
  39.3 28.8 %copy-start.1 = (f32[256,128]{1,0:T(8,128)}, f32[256,128]{1,0:T(8,128)S(1)}, u32[]{:S(2)}) copy-start(f32[256,128]{1,0:T(8,128)S(1)} %scatter_custom_fusion) | copy-start | bytes 393220
  39.4 28.6 %collective-permute-start.2 = (f32[7,64,128]{2,1,0:T(8,128)S(1)}, f32[7,64,128]{2,1,0:T(8,128)S(1)}, u32[]{:S(2)}, u32[]{:S(2)}) collective-permute-start(f32[7,64,128]{2,1,0:T(8,128)S(1)} %get-tuple-element.195), channel_id=1, source_target_pairs={{0,1},{1,2},{2,3},{3,4},{4,5},{5,6},{6,7},{7,8},{8,9},{9,10},{10,1... | collective-permute-start | bytes 688136 | tf_op jit(solution)/shard_map/ppermute | solution.py:18
  44.6 23.4 %collective-permute-start.3 = (f32[7,64,128]{2,1,0:T(8,128)S(1)}, f32[7,64,128]{2,1,0:T(8,128)S(1)}, u32[]{:S(2)}, u32[]{:S(2)}) collective-permute-start(f32[7,64,128]{2,1,0:T(8,128)S(1)} %get-tuple-element.196), channel_id=1, source_target_pairs={{1,0},{2,1},{3,2},{4,3},{5,4},{6,5},{7,6},{8,7},{9,8},{10,9},{11,1... | collective-permute-start | bytes 688136 | tf_op jit(solution)/shard_map/ppermute | solution.py:21
  49.0 18.3 %all-to-all-start = ((f32[7,32,8]{2,0,1:T(8,128)}), f32[7,32,8]{2,0,1:T(8,128)S(1)}, u32[]{:S(2)}, u32[]{:S(2)}) async-start(f32[7,32,8]{2,0,1:T(8,128)} %copy.63), calls=%async_computation | async-start | bytes 262144 | tf_op jit(solution)/shard_map/all_to_all | solution.py:182
where the time goes:
time: 87.7 us; the launch traced here: 87.4 us
  local copies, waits for them, and re-layouts  32 us (36%)
  other arithmetic  25.9 us (30%)
  starting transfers between devices  20.2 us (23%)
  waiting for transfers between devices  7.07 us (8%)
  between operations  1.79 us (2%)
    all_to_all x1, starting transfers between devices, local(): lax.all_to_all(outgoing, ('gx', 'gy'), split_axis=1, concat_axis=1, tiled...  10 us
    unnamed x25, local copies, waits for them, and re-layouts  9.81 us
    mul x4, other arithmetic, force_cell(): factor = other_mass[None] * (own_term + other_term)  8.53 us
    ppermute x2, starting transfers between devices, padded(): lax.ppermute(lax.slice_in_dim(block, block.shape[dim] - width, None, axis...  7.54 us
    all_to_all x1, waiting for transfers between devices, local(): lax.all_to_all(outgoing, ('gx', 'gy'), split_axis=1, concat_axis=1, tiled...  7.06 us
    gather x2, local copies, waits for them, and re-layouts, local(): positions.reshape(3, flat_count)[:, mig_source]  6.47 us
    reduce_sum x4, other arithmetic, density_cell(): jnp.sum(other_mass[None] * weights, axis=(1, 2))  5.79 us
    reduce_sum x8, other arithmetic, pair_geometry(): distance = jnp.sqrt(jnp.sum(separation * separation, axis=0))  5.34 us
  transfers between devices with their start and end apart: 5, of which 1 were waited for; matrix products, arithmetic and copies ran while one was open for 29% of the time, Pallas kernels for 0%

commit v1 on v0

--- a/solution.py
+++ b/solution.py
@@ -179,7 +179,10 @@
     slot_rank = jnp.sum(jnp.logical_and(same, earlier), axis=1)
     column = destination * capacity + slot_rank
     outgoing = jnp.zeros((7, devices * capacity), jnp.float32).at[:, column].set(payload)
-    arrivals = lax.all_to_all(outgoing, ("gx", "gy"), split_axis=1, concat_axis=1, tiled=True)
+    devices_2 = lax.axis_size(("gx", "gy"))
+    shards = jnp.stack(jnp.split(outgoing, devices_2, axis=1), axis=0)
+    shards = lax.all_to_all(shards, ("gx", "gy"), split_axis=0, concat_axis=0)
+    arrivals = jnp.concatenate(shards, axis=1)
     return (new_density, acceleration, arrivals)
 
 

time: 87.7 us -> 109 us (1.24)
  local copies, waits for them, and re-layouts: 32 us -> 52.6 us
    unnamed x25 -> x56, local copies, waits for them, and re-layouts: 9.81 us -> 28.1 us
    split x0 -> x34, local copies, waits for them, and re-layouts: none -> 2.6 us  [local(): shards = jnp.stack(jnp.split(outgoing, devices_2, axis=1), axis=0)]
    all_to_all x3 -> x0, local copies, waits for them, and re-layouts: 1.63 us -> none  [local(): lax.all_to_all(outgoing, ('gx', 'gy'), split_axis=1, concat_axis=1, tiled...]
  transfers between devices with their start and end apart: 5 -> 5, of which waited for: 1 -> 1; matrix products, arithmetic and copies ran while one was open for 29% -> 41% of each run, Pallas kernels for 0% -> 0%
where the time goes in v1:
time: 109 us; the launch traced here: 108 us
  local copies, waits for them, and re-layouts  52.6 us (48%)
  other arithmetic  25.9 us (24%)
  starting transfers between devices  20.7 us (19%)
  waiting for transfers between devices  6.88 us (6%)
  between operations  1.84 us (2%)
    unnamed x56, local copies, waits for them, and re-layouts  28.1 us
    all_to_all x1, starting transfers between devices, local(): shards = lax.all_to_all(shards, ('gx', 'gy'), split_axis=0, concat_axis=0)  9.9 us
    mul x4, other arithmetic, force_cell(): factor = other_mass[None] * (own_term + other_term)  8.53 us
    ppermute x2, starting transfers between devices, padded(): lax.ppermute(lax.slice_in_dim(block, block.shape[dim] - width, None, axis...  8.17 us
    all_to_all x1, waiting for transfers between devices, local(): shards = lax.all_to_all(shards, ('gx', 'gy'), split_axis=0, concat_axis=0)  6.87 us
    gather x2, local copies, waits for them, and re-layouts, local(): positions.reshape(3, flat_count)[:, mig_source]  6.47 us
    reduce_sum x4, other arithmetic, density_cell(): jnp.sum(other_mass[None] * weights, axis=(1, 2))  5.79 us
    reduce_sum x8, other arithmetic, pair_geometry(): distance = jnp.sqrt(jnp.sum(separation * separation, axis=0))  5.34 us
  transfers between devices with their start and end apart: 5, of which 1 were waited for; matrix products, arithmetic and copies ran while one was open for 41% of the time, Pallas kernels for 0%

profile of v1, /device:TPU:0, one launch (start us, length us, event | category | flops | bytes accessed | tf_op | source)
XLA Modules:
  0.0 108.4 jit_solution(10974316959996240766)
XLA Ops:
  0.7 1.1 %pad_maximum_fusion.5 = (f32[4,64,128]{2,1,0:T(8,128)S(1)}, f32[4,64,128]{2,1,0:T(8,128)S(1)}) fusion(f32[1,256,128]{2,1,0:T(8,128)} %bitcast.173, f32[3,256,128]{2,1,0:T(8,128)} %param.16), kind=kLoop, calls=%fused_computation.73 | loop fusion | flops 65536 | bytes 786432 | tf_op jit(solution)/shard_map/slice | solution.py:19
  1.8 1.3 %collective-permute-start.1 = (f32[4,64,128]{2,1,0:T(8,128)S(1)}, f32[4,64,128]{2,1,0:T(8,128)S(1)}, u32[]{:S(2)}, u32[]{:S(2)}) collective-permute-start(f32[4,64,128]{2,1,0:T(8,128)S(1)} %get-tuple-element.215), channel_id=1, source_target_pairs={{1,0},{2,1},{3,2},{4,3},{5,4},{6,5},{7,6},{8,7},{9,8},{10,9},{11,1... | collective-permute-start | bytes 393224 | tf_op jit(solution)/shard_map/ppermute | solution.py:21
  3.1 3.0 %collective-permute-start = (f32[4,64,128]{2,1,0:T(8,128)S(1)}, f32[4,64,128]{2,1,0:T(8,128)S(1)}, u32[]{:S(2)}, u32[]{:S(2)}) collective-permute-start(f32[4,64,128]{2,1,0:T(8,128)S(1)} %get-tuple-element.214), channel_id=1, source_target_pairs={{0,1},{1,2},{2,3},{3,4},{4,5},{5,6},{6,7},{7,8},{8,9},{9,10},{10,1... | collective-permute-start | bytes 393224 | tf_op jit(solution)/shard_map/ppermute | solution.py:18
  6.2 1.0 constant_dynamic-update-slice_fusion.1
  9.5 8.7 %copy.264 = f32[3,256,128]{0,2,1:T(8,128)} copy(f32[3,256,128]{2,1,0:T(8,128)S(1)} %copy-done) | data formatting | bytes 786432 | tf_op args[0]
  18.3 6.4 %gather_fusion.9 = f32[128,3]{1,0:T(8,128)S(1)} fusion(f32[3,32768]{0,1:T(8,128)} %bitcast.171, s32[1024]{0:T(1024)S(1)} %pad_clamp_fusion), kind=kCustom, calls=%fused_computation.12 | custom fusion | bytes 3584 | tf_op jit(solution)/shard_map/gather | solution.py:168
  24.7 1.2 %gather_fusion.10 = f32[128]{0:T(128)S(1)} fusion(f32[32768]{0:T(1024)S(1)} %bitcast.174, s32[1024]{0:T(1024)S(1)} %pad_clamp_fusion), kind=kCustom, calls=%fused_computation.13 | custom fusion | bytes 1536 | tf_op jit(solution)/shard_map/gather | solution.py:169
  25.9 1.1 %gather_fusion.11 = f32[128]{0:T(128)S(1)} fusion(f32[32768]{0:T(1024)S(1)} %bitcast.177, s32[1024]{0:T(1024)S(1)} %pad_clamp_fusion), kind=kCustom, calls=%fused_computation.14 | custom fusion | bytes 1536 | tf_op jit(solution)/shard_map/gather | solution.py:170
  27.1 1.1 %gather_fusion.12 = f32[128]{0:T(128)S(1)} fusion(f32[32768]{0:T(1024)S(1)} %bitcast.178, s32[1024]{0:T(1024)S(1)} %pad_clamp_fusion), kind=kCustom, calls=%fused_computation.15 | custom fusion | bytes 1536 | tf_op jit(solution)/shard_map/gather | solution.py:171
  29.4 0.7 gather_fusion.14
  30.2 9.0 %while.20 = (s32[]{:T(128)}, f32[4,128]{1,0:T(4,128)S(1)}, f32[4,27,128]{2,1,0:T(8,128)S(1)}, f32[4,3,128]{2,1,0:T(4,128)S(1)}, f32[4,3,27,128]{3,2,0,1:T(8,128)...) while((s32[]{:T(128)}, f32[4,128]{1,0:T(4,128)S(1)}, f32[4,27,128]{2,1,0:T(8,128)S(1)}, ...), condition=%wide.region_3.5_spmd, body=%wide.region_0.4_spmd.sunk | while | flops 10617218 | bytes 3714165 | solution.py:106
  31.0 1.4 %fusion.42 = f32[128]{0:T(128)S(1)} fusion(f32[128,27,128]{2,0,1:T(8,128)S(1)} %multiply_reduce_fusion.2, f32[128]{0:T(128)S(1)} %fusion.41, f32[27,128]{1,0:T(8,128)S(1)} %dynamic-slice_bitcast_fusion.12), kind=kLoop, calls=%fused_computation.27.clone.1 | loop fusion | flops 7077760 | bytes 1784320 | tf_op jit(solution)/shard_map/while/body/eval_jaxpr/reduce_sum | solution.py:53
  33.3 1.4 %fusion.42 = f32[128]{0:T(128)S(1)} fusion(f32[128,27,128]{2,0,1:T(8,128)S(1)} %multiply_reduce_fusion.2, f32[128]{0:T(128)S(1)} %fusion.41, f32[27,128]{1,0:T(8,128)S(1)} %dynamic-slice_bitcast_fusion.12), kind=kLoop, calls=%fused_computation.27.clone.1 | loop fusion | flops 7077760 | bytes 1784320 | tf_op jit(solution)/shard_map/while/body/eval_jaxpr/reduce_sum | solution.py:53
  35.5 1.4 %fusion.42 = f32[128]{0:T(128)S(1)} fusion(f32[128,27,128]{2,0,1:T(8,128)S(1)} %multiply_reduce_fusion.2, f32[128]{0:T(128)S(1)} %fusion.41, f32[27,128]{1,0:T(8,128)S(1)} %dynamic-slice_bitcast_fusion.12), kind=kLoop, calls=%fused_computation.27.clone.1 | loop fusion | flops 7077760 | bytes 1784320 | tf_op jit(solution)/shard_map/while/body/eval_jaxpr/reduce_sum | solution.py:53
  37.8 1.4 %fusion.42 = f32[128]{0:T(128)S(1)} fusion(f32[128,27,128]{2,0,1:T(8,128)S(1)} %multiply_reduce_fusion.2, f32[128]{0:T(128)S(1)} %fusion.41, f32[27,128]{1,0:T(8,128)S(1)} %dynamic-slice_bitcast_fusion.12), kind=kLoop, calls=%fused_computation.27.clone.1 | loop fusion | flops 7077760 | bytes 1784320 | tf_op jit(solution)/shard_map/while/body/eval_jaxpr/reduce_sum | solution.py:53
  39.3 0.7 scatter_custom_fusion
  40.0 1.1 %gather_fusion.13 = f32[128]{0:T(128)S(1)} fusion(f32[32768]{0:T(1024)S(1)} %bitcast.172, s32[1024]{0:T(1024)S(1)} %pad_clamp_fusion), kind=kCustom, calls=%fused_computation.16 | custom fusion | bytes 1536 | tf_op jit(solution)/shard_map/gather | solution.py:172
  41.3 0.9 scatter_custom_fusion.1
  42.4 1.3 %collective-permute-start.3 = (f32[7,64,128]{2,1,0:T(8,128)S(1)}, f32[7,64,128]{2,1,0:T(8,128)S(1)}, u32[]{:S(2)}, u32[]{:S(2)}) collective-permute-start(f32[7,64,128]{2,1,0:T(8,128)S(1)} %get-tuple-element.213), channel_id=1, source_target_pairs={{1,0},{2,1},{3,2},{4,3},{5,4},{6,5},{7,6},{8,7},{9,8},{10,9},{11,1... | collective-permute-start | bytes 688136 | tf_op jit(solution)/shard_map/ppermute | solution.py:21
  43.7 5.1 %collective-permute-start.2 = (f32[7,64,128]{2,1,0:T(8,128)S(1)}, f32[7,64,128]{2,1,0:T(8,128)S(1)}, u32[]{:S(2)}, u32[]{:S(2)}) collective-permute-start(f32[7,64,128]{2,1,0:T(8,128)S(1)} %get-tuple-element.212), channel_id=1, source_target_pairs={{0,1},{1,2},{2,3},{3,4},{4,5},{5,6},{6,7},{7,8},{8,9},{9,10},{10,1... | collective-permute-start | bytes 688136 | tf_op jit(solution)/shard_map/ppermute | solution.py:18
  70.3 9.9 %all-to-all-start = ((f32[32,7,8]{2,1,0:T(8,128)}), f32[32,7,8]{2,1,0:T(8,128)S(1)}, u32[]{:S(2)}, u32[]{:S(2)}) async-start(f32[32,7,8]{2,1,0:T(8,128)} %constant_dynamic-update-slice_fusion.2), calls=%async_computation | async-start | bytes 262144 | tf_op jit(solution)/shard_map/all_to_all | solution.py:184
  81.4 6.9 %all-to-all-done = f32[32,7,8]{2,1,0:T(8,128)S(1)} async-done(((f32[32,7,8]{2,1,0:T(8,128)}), f32[32,7,8]{2,1,0:T(8,128)S(1)}, u32[]{:S(2)}, u32[]{:S(2)}) %all-to-all-start) | async-done | bytes 7200 | tf_op jit(solution)/shard_map/all_to_all | solution.py:184
  88.3 0.7 reshape.260
  90.3 0.7 gather_fusion.15
  93.1 14.6 %while.21 = (s32[]{:T(128)}, f32[4,3,128]{2,0,1:T(4,128)S(1)}, f32[4,27,128]{2,1,0:T(8,128)S(1)}, f32[4,128]{1,0:T(4,128)S(1)}, f32[4,128]{1,0:T(4,128)S(1)}, /*...) while((s32[]{:T(128)}, f32[4,3,128]{2,0,1:T(4,128)S(1)}, ...), condition=%wide.region_8.10_spmd, body=%wide.region_5.9_spmd.sunk | while | flops 19931648 | bytes 7402649 | solution.py:146
  93.8 2.1 %add_multiply_fusion.2 = f32[128,27,128]{2,0,1:T(8,128)S(1)} fusion(f32[128,27,128]{2,0,1:T(8,128)S(1)} %fusion.45, f32[27,128]{1,0:T(8,128)S(1)} %get-tuple-element.361, f32[27,128]{1,0:T(8,128)S(1)} %get-tuple-element.362, f32[128]{0:T(128)S(1)} %get-tuple-element.363, f32[128]{0:T(128)S(1)} %get-tuple-element.364, f32[27,128]{1,0:T(8,128)S(1)} %get-tuple-element.365), kind=kLoop, calls=%fused_computation.42.clone.1 | loop fusion | flops 12386304 | bytes 3581440 | tf_op jit(solution)/shard_map/while/body/eval_jaxpr/mul | solution.py:66
  96.0 0.7 fusion.46
  97.5 2.1 %add_multiply_fusion.2 = f32[128,27,128]{2,0,1:T(8,128)S(1)} fusion(f32[128,27,128]{2,0,1:T(8,128)S(1)} %fusion.45, f32[27,128]{1,0:T(8,128)S(1)} %get-tuple-element.361, f32[27,128]{1,0:T(8,128)S(1)} %get-tuple-element.362, f32[128]{0:T(128)S(1)} %get-tuple-element.363, f32[128]{0:T(128)S(1)} %get-tuple-element.364, f32[27,128]{1,0:T(8,128)S(1)} %get-tuple-element.365), kind=kLoop, calls=%fused_computation.42.clone.1 | loop fusion | flops 12386304 | bytes 3581440 | tf_op jit(solution)/shard_map/while/body/eval_jaxpr/mul | solution.py:66
  99.6 0.7 fusion.46
  101.1 2.1 %add_multiply_fusion.2 = f32[128,27,128]{2,0,1:T(8,128)S(1)} fusion(f32[128,27,128]{2,0,1:T(8,128)S(1)} %fusion.45, f32[27,128]{1,0:T(8,128)S(1)} %get-tuple-element.361, f32[27,128]{1,0:T(8,128)S(1)} %get-tuple-element.362, f32[128]{0:T(128)S(1)} %get-tuple-element.363, f32[128]{0:T(128)S(1)} %get-tuple-element.364, f32[27,128]{1,0:T(8,128)S(1)} %get-tuple-element.365), kind=kLoop, calls=%fused_computation.42.clone.1 | loop fusion | flops 12386304 | bytes 3581440 | tf_op jit(solution)/shard_map/while/body/eval_jaxpr/mul | solution.py:66
  103.3 0.7 fusion.46
  104.8 2.1 %add_multiply_fusion.2 = f32[128,27,128]{2,0,1:T(8,128)S(1)} fusion(f32[128,27,128]{2,0,1:T(8,128)S(1)} %fusion.45, f32[27,128]{1,0:T(8,128)S(1)} %get-tuple-element.361, f32[27,128]{1,0:T(8,128)S(1)} %get-tuple-element.362, f32[128]{0:T(128)S(1)} %get-tuple-element.363, f32[128]{0:T(128)S(1)} %get-tuple-element.364, f32[27,128]{1,0:T(8,128)S(1)} %get-tuple-element.365), kind=kLoop, calls=%fused_computation.42.clone.1 | loop fusion | flops 12386304 | bytes 3581440 | tf_op jit(solution)/shard_map/while/body/eval_jaxpr/mul | solution.py:66
  (201 shorter events, 36.5 us)
Async XLA Ops:
  0.6 6.7 %copy-start = (f32[3,256,128]{2,1,0:T(8,128)S(1)}, f32[3,256,128]{2,1,0:T(8,128)}, u32[]{:S(2)}) copy-start(f32[3,256,128]{2,1,0:T(8,128)} %param.16) | copy-start | bytes 1179652
  0.6 8.0 %copy-start.3 = (f32[256,128]{1,0:T(8,128)S(1)}, f32[256,128]{1,0:T(8,128)}, u32[]{:S(2)}) copy-start(f32[256,128]{1,0:T(8,128)} %param.17) | copy-start | bytes 393220
  0.7 8.3 %copy-start.4 = (f32[256,128]{1,0:T(8,128)S(1)}, f32[256,128]{1,0:T(8,128)}, u32[]{:S(2)}) copy-start(f32[256,128]{1,0:T(8,128)} %param.18) | copy-start | bytes 393220
  0.7 6.6 %copy-start.7 = (s32[4]{0:T(128)S(1)}, s32[4]{0:T(128)}, u32[]{:S(2)}) copy-start(s32[4]{0:T(128)} %param.21) | copy-start | bytes 52
  0.7 6.6 %copy-start.6 = (s32[4,27]{1,0:T(4,128)S(1)}, s32[4,27]{1,0:T(4,128)}, u32[]{:S(2)}) copy-start(s32[4,27]{1,0:T(4,128)} %param.23) | copy-start | bytes 1300
  0.7 8.1 %copy-start.9 = (s32[128]{0:T(128)S(1)}, s32[128]{0:T(128)}, u32[]{:S(2)}) copy-start(s32[128]{0:T(128)} %param.24) | copy-start | bytes 1540
  0.7 7.9 %copy-start.8 = (s32[128,1]{0,1:T(1,128)S(1)}, s32[128,1]{0,1:T(1,128)}, u32[]{:S(2)}) copy-start(s32[128,1]{0,1:T(1,128)} %param.25) | copy-start | bytes 1540
  1.8 26.4 %collective-permute-start.1 = (f32[4,64,128]{2,1,0:T(8,128)S(1)}, f32[4,64,128]{2,1,0:T(8,128)S(1)}, u32[]{:S(2)}, u32[]{:S(2)}) collective-permute-start(f32[4,64,128]{2,1,0:T(8,128)S(1)} %get-tuple-element.215), channel_id=1, source_target_pairs={{1,0},{2,1},{3,2},{4,3},{5,4},{6,5},{7,6},{8,7},{9,8},{10,9},{11,1... | collective-permute-start | bytes 393224 | tf_op jit(solution)/shard_map/ppermute | solution.py:21
  3.1 25.2 %collective-permute-start = (f32[4,64,128]{2,1,0:T(8,128)S(1)}, f32[4,64,128]{2,1,0:T(8,128)S(1)}, u32[]{:S(2)}, u32[]{:S(2)}) collective-permute-start(f32[4,64,128]{2,1,0:T(8,128)S(1)} %get-tuple-element.214), channel_id=1, source_target_pairs={{0,1},{1,2},{2,3},{3,4},{4,5},{5,6},{6,7},{7,8},{8,9},{9,10},{10,1... | collective-permute-start | bytes 393224 | tf_op jit(solution)/shard_map/ppermute | solution.py:18
  9.5 17.5 %copy-start.5 = (f32[256,128]{1,0:T(8,128)S(1)}, f32[256,128]{1,0:T(8,128)}, u32[]{:S(2)}) copy-start(f32[256,128]{1,0:T(8,128)} %param.19) | copy-start | bytes 393220
  30.2 9.0 %copy-start.2 = (f32[256,128]{1,0:T(8,128)S(1)}, f32[256,128]{1,0:T(8,128)}, u32[]{:S(2)}) copy-start(f32[256,128]{1,0:T(8,128)} %param.20) | copy-start | bytes 393220
  40.0 40.3 %copy-start.1 = (f32[256,128]{1,0:T(8,128)}, f32[256,128]{1,0:T(8,128)S(1)}, u32[]{:S(2)}) copy-start(f32[256,128]{1,0:T(8,128)S(1)} %scatter_custom_fusion) | copy-start | bytes 393220
  42.4 46.6 %collective-permute-start.3 = (f32[7,64,128]{2,1,0:T(8,128)S(1)}, f32[7,64,128]{2,1,0:T(8,128)S(1)}, u32[]{:S(2)}, u32[]{:S(2)}) collective-permute-start(f32[7,64,128]{2,1,0:T(8,128)S(1)} %get-tuple-element.213), channel_id=1, source_target_pairs={{1,0},{2,1},{3,2},{4,3},{5,4},{6,5},{7,6},{8,7},{9,8},{10,9},{11,1... | collective-permute-start | bytes 688136 | tf_op jit(solution)/shard_map/ppermute | solution.py:21
  43.7 45.3 %collective-permute-start.2 = (f32[7,64,128]{2,1,0:T(8,128)S(1)}, f32[7,64,128]{2,1,0:T(8,128)S(1)}, u32[]{:S(2)}, u32[]{:S(2)}) collective-permute-start(f32[7,64,128]{2,1,0:T(8,128)S(1)} %get-tuple-element.212), channel_id=1, source_target_pairs={{0,1},{1,2},{2,3},{3,4},{4,5},{5,6},{6,7},{7,8},{8,9},{9,10},{10,1... | collective-permute-start | bytes 688136 | tf_op jit(solution)/shard_map/ppermute | solution.py:18
  70.3 17.9 %all-to-all-start = ((f32[32,7,8]{2,1,0:T(8,128)}), f32[32,7,8]{2,1,0:T(8,128)S(1)}, u32[]{:S(2)}, u32[]{:S(2)}) async-start(f32[32,7,8]{2,1,0:T(8,128)} %constant_dynamic-update-slice_fusion.2), calls=%async_computation | async-start | bytes 262144 | tf_op jit(solution)/shard_map/all_to_all | solution.py:184
